TPU v7x, 256 devices: a whole 4x4x8 slice. The times are simulated.
256 devices in a mesh: dp: 4 (over x), space: 64 (over y, z, core).
Axes of the slice: x: 4, y: 4, z: 8, core: 2. Of those that a mesh axis runs over, the one named last changes fastest.
Arguments:
- volume: bfloat16 [4, 128, 128, 16, 256], P('dp', None, 'space'), may hold values from -6 to 6
- w_first: bfloat16 [3, 3, 3, 128, 256], replicated, may hold values from -0.109375 to 0.109375
- w_second: bfloat16 [3, 3, 3, 256, 512], P(None, None, None, 'space'), may hold values from -0.078125 to 0.078125
- cotangent: bfloat16 [4, 512, 32, 256], P('dp', 'space'), may hold values from -6 to 6
Outputs:
- grad_second: float32 [3, 3, 3, 256, 512], P(None, None, None, 'space')
- pre_grad: bfloat16 [4, 256, 64, 4, 256], P('dp', None, 'space')
All inputs are finite; a program needn't handle non-finite values.
Results may differ from a plain program's by a relative error of at most 0.0049.
Values may be sent and summed in bfloat16 or wider, within the bound.
No kernel may reach another device: no remote copies, remote signals or barrier semaphores. Data moves between devices by JAX's collectives and lax.ppermute only.
A program may use at most 128 MiB of HBM per device.

v0:
```python
import jax
import jax.numpy as jnp
from jax import lax
from jax.sharding import PartitionSpec as P

C3 = 512
WID = 128
leak_slope = 0.3


def from_behind(block, axis, distance):
    devices = range(lax.axis_size(axis))
    route = [(i - distance, i) for i in devices if i - distance in devices]
    return lax.ppermute(block, axis, route)


def activate(values):
    return leak_slope * values + (1.0 - leak_slope) * values * jax.nn.sigmoid(values)


def slope_of(values):
    sigmoid_value = jax.nn.sigmoid(values)
    return leak_slope + (1.0 - leak_slope) * (
        sigmoid_value + values * sigmoid_value * (1.0 - sigmoid_value)
    )


def stride_taps(values, along_dim):
    length = values.shape[along_dim] // 2
    paired = values.reshape(values.shape[:along_dim] + (length, 2) + values.shape[along_dim + 1 :])
    even_cells = lax.index_in_dim(paired, 0, along_dim + 1, keepdims=False)
    odd_cells = lax.index_in_dim(paired, 1, along_dim + 1, keepdims=False)
    before = jnp.concatenate(
        [
            jnp.zeros_like(lax.slice_in_dim(odd_cells, 0, 1, axis=along_dim)),
            lax.slice_in_dim(odd_cells, 0, length - 1, axis=along_dim),
        ],
        along_dim,
    )
    return [before, even_cells, odd_cells]


def step_cells(values, by_row, by_col, row_len):
    cells = values.shape[-1]
    if by_row:
        filler = jnp.zeros(values.shape[:-1] + (row_len,), values.dtype)
        values = jnp.concatenate([filler, values[..., : cells - row_len]], -1)
    if by_col:
        filler = jnp.zeros(values.shape[:-1] + (1,), values.dtype)
        moved = jnp.concatenate([filler, values[..., : cells - 1]], -1)
        keeper = lax.iota(jnp.int32, cells) % row_len != 0
        values = jnp.where(keeper, moved, jnp.zeros_like(moved))
    return values


def plane_taps(values, row_len):
    phases = values.shape[-2]
    out_phases = phases // 2
    collected = []
    for row_tap in range(3):
        for col_tap in range(3):
            rows_out = []
            for row_phase in range(out_phases):
                cols_out = []
                for col_phase in range(out_phases):
                    row_at = 2 * row_phase + row_tap - 1
                    col_at = 2 * col_phase + col_tap - 1
                    part = values[..., row_at % phases, col_at % phases, :]
                    cols_out.append(step_cells(part, row_at < 0, col_at < 0, row_len))
                rows_out.append(jnp.stack(cols_out, -2))
            collected.append(jnp.stack(rows_out, -3))
    return collected


def all_taps(values, row_len):
    collected = []
    for depth_part in stride_taps(values, 1):
        collected.extend(plane_taps(depth_part, row_len))
    return collected


def contract_first(left_side, right_side):
    return lax.dot_general(
        left_side, right_side, (((0,), (0,)), ((), ())), preferred_element_type=jnp.float32
    )


def contract_last(left_side, right_side):
    return lax.dot_general(
        left_side, right_side, (((1,), (1,)), ((), ())), preferred_element_type=jnp.float32
    )


def per_device(volume, w_first, w_second, cotangent):
    channels = volume.shape[1]
    depth_cells = volume.shape[2]
    cell_count = volume.shape[4]
    half_depth = depth_cells // 2
    out_channels = w_first.shape[4]
    row_len = WID // 4
    paired = volume[0].reshape(channels, half_depth, 2, 4, 4, cell_count)
    even_cells = paired[:, :, 0]
    odd_cells = paired[:, :, 1]
    w_flat = w_first.reshape(27 * channels, out_channels)
    rim_cells = from_behind(odd_cells, "space", 1)
    before = jnp.concatenate([rim_cells, odd_cells[:, : half_depth - 1]], 1)
    collected = []
    for depth_part in (before, even_cells, odd_cells):
        collected.extend(plane_taps(depth_part, row_len))
    stacked = jnp.stack(collected, 0).reshape(27 * channels, -1)
    pre_act = contract_first(w_flat, stacked).reshape(out_channels, half_depth, 4, cell_count)
    hidden = activate(pre_act).astype(jnp.bfloat16)
    by_channel = lax.all_to_all(hidden, "space", split_axis=0, concat_axis=1, tiled=True)
    own_channels = by_channel.shape[0]
    full_depth = by_channel.shape[1]
    hidden_cells = by_channel.reshape(own_channels, full_depth, 2, 2, cell_count)
    hidden_taps = jnp.stack(all_taps(hidden_cells, row_len), 0).reshape(27 * own_channels, -1)
    w_rows = w_second.reshape(27 * own_channels, C3)
    out_cells = hidden_taps.shape[1]
    gathered = lax.all_gather(cotangent[0], "space", axis=0, tiled=True)
    cot_flat = gathered.reshape(C3, out_cells)
    weight_grad = contract_last(hidden_taps, cot_flat)
    tap_terms = jnp.dot(w_rows, cot_flat, preferred_element_type=jnp.float32)
    grad_second = lax.psum(weight_grad, "dp").reshape(3, 3, 3, own_channels, C3)

    def spread(field):
        return jnp.stack(all_taps(field, row_len), 0).reshape(27 * own_channels, -1)

    unused, pull = jax.vjp(
        spread, jnp.zeros((own_channels, full_depth, 2, 2, cell_count), jnp.float32)
    )
    back_terms = pull(tap_terms)[0]
    back_terms = back_terms.astype(jnp.bfloat16).reshape(own_channels, full_depth, 4, cell_count)
    hidden_grad = lax.all_to_all(back_terms, "space", split_axis=1, concat_axis=0, tiled=True)
    pre_grad = (hidden_grad.astype(jnp.float32) * slope_of(pre_act)).astype(jnp.bfloat16)
    return (grad_second, pre_grad[None])


def solution(mesh):
    in_specs = (
        P("dp", None, "space", None, None),
        P(),
        P(None, None, None, "space", None),
        P("dp", "space", None, None),
    )
    out_specs = (P(None, None, None, "space", None), P("dp", None, "space", None, None))
    return jax.shard_map(
        per_device, mesh=mesh, in_specs=in_specs, out_specs=out_specs, check_vma=False
    )
```

profile of v0, /device:TPU:8, one launch (start us, length us, event | category | flops | bytes accessed | tf_op | source)
XLA Modules:
  0.0 217.8 jit_solution(14263887980538199394)
XLA Ops:
  7.9 2.8 %copy.103 = bf16[1,128,2,16,256]{4,1,3,2,0:T(8,128)(2,1)S(1)} copy(bf16[1,128,2,16,256]{4,3,2,1,0:T(8,128)(2,1)} %param.4) | data formatting | bytes 4194304 | tf_op args[0]
  10.9 1.9 collective-permute-start
  14.1 16.5 %collective-permute-done = bf16[128,1,4,4,256]{4,0,3,2,1:T(8,128)(2,1)S(1)} collective-permute-done((bf16[128,1,4,4,256]{4,0,3,2,1:T(8,128)(2,1)S(1)}, bf16[128,1,4,4,256]{4,0,3,2,1:T(8,128)(2,1)S(1)}, u32[]{:S(2)}, u32[]{:S(2)}) %collective-permute-start) | collective-permute-done | bytes 1048608 | tf_op jit(solution)/shard_map/ppermute | solution.py:14
  32.8 6.8 %copy.104 = bf16[27,128,1,2,2,256]{5,4,3,1,0,2:T(2,128)(2,1)} copy(bf16[27,128,1,2,2,256]{5,1,4,3,2,0:T(8,128)(2,1)S(1)} %fusion.33) | data formatting | bytes 14155776 | tf_op jit(solution)/shard_map/stack | solution.py:110
  39.6 16.2 %reshape.233 = bf16[3456,1024]{1,0:T(8,128)(2,1)} reshape(bf16[27,128,1,2,2,256]{5,4,3,1,0,2:T(2,128)(2,1)} %copy.104) | data formatting | bytes 14155776 | tf_op jit(solution)/shard_map/reshape | solution.py:110
  55.8 6.2 %fusion.2 = (bf16[256,1024]{0,1:T(8,128)(2,1)S(1)}, f32[1024,256]{1,0:T(8,128)}) fusion(bf16[3456,1024]{1,0:T(8,128)(2,1)} %reshape.233, bf16[3456,256]{1,0:T(8,128)(2,1)S(1)} %bitcast.641), kind=kOutput, calls=%fused_computation.9 | convolution fusion | flops 1814036480 | bytes 10420224 | tf_op jit(solution)/shard_map/dot_general | solution.py:83
  62.0 1.1 copy.105
  63.0 10.7 %all-to-all-start = ((bf16[256,1,4,256]{3,2,1,0:T(4,128)(2,1)}), bf16[256,1,4,256]{3,2,1,0:T(4,128)(2,1)S(1)}, u32[]{:S(2)}, u32[]{:S(2)}) async-start(bf16[256,1,4,256]{3,2,1,0:T(4,128)(2,1)} %copy.105), calls=%async_computation | async-start | bytes 1048576 | tf_op jit(solution)/shard_map/all_to_all | solution.py:113
  73.9 1.6 copy.142
  75.5 20.0 %all-to-all-done = bf16[256,1,4,256]{3,2,1,0:T(4,128)(2,1)S(1)} async-done(((bf16[256,1,4,256]{3,2,1,0:T(4,128)(2,1)}), bf16[256,1,4,256]{3,2,1,0:T(4,128)(2,1)S(1)}, u32[]{:S(2)}, u32[]{:S(2)}) %all-to-all-start) | async-done | bytes 524320 | tf_op jit(solution)/shard_map/all_to_all | solution.py:113
  96.4 0.7 constant_dynamic-update-slice_fusion.26
  107.2 0.7 constant_dynamic-update-slice_fusion.11
  114.3 16.7 %copy.149 = bf16[64,8,32,256]{3,1,2,0:T(8,128)(2,1)} copy(bf16[64,8,32,256]{3,2,1,0:T(8,128)(2,1)} %bitcast.644) | data formatting | bytes 16777216
  131.0 4.7 %fusion.42 = f32[108,8192]{1,0:T(8,128)S(1)} fusion(bf16[108,512]{1,0:T(8,128)(2,1)S(1)} %reshape.238, bf16[512,8192]{1,0:T(8,128)(2,1)} %bitcast.642), kind=kOutput, calls=%fused_computation.302 | convolution fusion | flops 905969664 | bytes 12038144 | tf_op jit(solution)/shard_map/dot_general | solution.py:123
  139.5 1.1 copy.140
  140.6 7.1 %all-to-all-start.1 = ((bf16[4,64,4,256]{3,0,2,1:T(4,128)(2,1)}), bf16[4,64,4,256]{3,0,2,1:T(4,128)(2,1)S(1)}, u32[]{:S(2)}, u32[]{:S(2)}) async-start(bf16[4,64,4,256]{3,0,2,1:T(4,128)(2,1)} %bitcast.260), calls=%async_computation.1 | async-start | bytes 1048576 | tf_op jit(solution)/shard_map/all_to_all | solution.py:134
  149.3 1.8 copy.111
  151.3 1.2 copy.150
  152.5 7.1 %fusion.41 = f32[108,512]{1,0:T(8,128)} fusion(bf16[108,8192]{1,0:T(8,128)(2,1)S(1)} %bitcast.646, bf16[512,8192]{1,0:T(8,128)(2,1)} %bitcast.643), kind=kOutput, calls=%fused_computation.301 | convolution fusion | flops 905969664 | bytes 10379264 | tf_op jit(solution)/shard_map/dot_general | solution.py:89
  159.7 1.7 reshape.237
  161.4 3.0 %all-to-all-done.1 = bf16[4,64,4,256]{3,0,2,1:T(4,128)(2,1)S(1)} async-done(((bf16[4,64,4,256]{3,0,2,1:T(4,128)(2,1)}), bf16[4,64,4,256]{3,0,2,1:T(4,128)(2,1)S(1)}, u32[]{:S(2)}, u32[]{:S(2)}) %all-to-all-start.1) | async-done | bytes 524320 | tf_op jit(solution)/shard_map/all_to_all | solution.py:134
  164.9 1.8 fusion
  166.7 42.7 %all-reduce.93.cloned.1.call-done = f32[3,3,3,4,512]{4,3,2,1,0:T(4,128)} async-done(((f32[3,3,3,4,512]{4,3,2,1,0:T(4,128)}), f32[3,3,3,4,512]{4,3,2,1,0:T(4,128)}) %all-reduce.93.cloned.1.call-update) | async-done | bytes 221200 | tf_op jit(solution)/shard_map/psum | solution.py:124
  209.4 1.6 copy.206
  (146 shorter events, 27.2 us)
Async XLA Ops:
  7.2 48.6 %copy-start = (bf16[3,3,3,128,256]{4,3,2,1,0:T(8,128)(2,1)S(1)}, bf16[3,3,3,128,256]{4,3,2,1,0:T(8,128)(2,1)}, u32[]{:S(2)}) copy-start(bf16[3,3,3,128,256]{4,3,2,1,0:T(8,128)(2,1)} %param.5) | copy-start | bytes 5308420
  7.2 107.1 %all-gather.3.cloned.1.call-start = ((), (), s32[]{:S(2)}) async-start(), calls=%async_computation.3 | async-start | bytes 8519680 | tf_op jit(solution)/shard_map/all_gather | solution.py:120
  10.9 19.7 %collective-permute-start = (bf16[128,1,4,4,256]{4,0,3,2,1:T(8,128)(2,1)S(1)}, bf16[128,1,4,4,256]{4,0,3,2,1:T(8,128)(2,1)S(1)}, u32[]{:S(2)}, u32[]{:S(2)}) collective-permute-start(bf16[128,1,4,4,256]{4,0,3,2,1:T(8,128)(2,1)S(1)} %get-tuple-element.34), channel_id=1, source_target_pairs={{0,1},{1,2},{2,3},{3,4},{4,5},{5,6},{6,7},{7,8},{8,9},{9,10},{10,1... | collective-permute-start | bytes 3145736 | tf_op jit(solution)/shard_map/ppermute | solution.py:14
  55.8 18.1 %copy-start.2 = (bf16[3,3,3,4,512]{4,3,2,1,0:T(4,128)(2,1)S(1)}, bf16[3,3,3,4,512]{4,3,2,1,0:T(4,128)(2,1)}, u32[]{:S(2)}) copy-start(bf16[3,3,3,4,512]{4,3,2,1,0:T(4,128)(2,1)} %param.6) | copy-start | bytes 331780
  63.0 32.5 %all-to-all-start = ((bf16[256,1,4,256]{3,2,1,0:T(4,128)(2,1)}), bf16[256,1,4,256]{3,2,1,0:T(4,128)(2,1)S(1)}, u32[]{:S(2)}, u32[]{:S(2)}) async-start(bf16[256,1,4,256]{3,2,1,0:T(4,128)(2,1)} %copy.105), calls=%async_computation | async-start | bytes 1048576 | tf_op jit(solution)/shard_map/all_to_all | solution.py:113
  140.6 23.8 %all-to-all-start.1 = ((bf16[4,64,4,256]{3,0,2,1:T(4,128)(2,1)}), bf16[4,64,4,256]{3,0,2,1:T(4,128)(2,1)S(1)}, u32[]{:S(2)}, u32[]{:S(2)}) async-start(bf16[4,64,4,256]{3,0,2,1:T(4,128)(2,1)} %bitcast.260), calls=%async_computation.1 | async-start | bytes 1048576 | tf_op jit(solution)/shard_map/all_to_all | solution.py:134
  147.7 61.7 %all-reduce.93.cloned.1.call-start = ((), (), s32[]{:S(2)}) async-start(), calls=%async_computation.2 | async-start | bytes 442368 | tf_op jit(solution)/shard_map/psum | solution.py:124
  152.5 58.5 %copy-start.1 = (bf16[3,3,3,128,256]{4,3,2,1,0:T(8,128)(2,1)S(1)}, bf16[3,3,3,128,256]{4,3,2,1,0:T(8,128)(2,1)}, u32[]{:S(2)}) copy-start(bf16[3,3,3,128,256]{4,3,2,1,0:T(8,128)(2,1)} %param.5) | copy-start | bytes 5308420
Sparse Core Ops, SparseCore 0:
  10.8 93.5 all-gather.2
  161.5 47.8 all-reduce.92
where the time goes:
time: 219 us; the launch traced here: 218 us
  waiting for transfers between devices  82.9 us (38%)
  local copies, waits for them, and re-layouts  70.2 us (32%)
  starting transfers between devices  20.1 us (9%)
  matrix products  18 us (8%)
  between operations  14.9 us (7%)
  other arithmetic  11.8 us (5%)
    psum x1, waiting for transfers between devices, per_device(): grad_second = lax.psum(weight_grad, 'dp').reshape(3, 3, 3, own_channels, C3)  42.7 us
    unnamed x29, local copies, waits for them, and re-layouts  34.1 us
    all_to_all x1, waiting for transfers between devices, per_device(): lax.all_to_all(hidden, 'space', split_axis=0, concat_axis=1, tiled=True)  20 us
    ppermute x1, waiting for transfers between devices, from_behind(): return lax.ppermute(block, axis, route)  16.5 us
    reshape x1, local copies, waits for them, and re-layouts, per_device(): stacked = jnp.stack(collected, 0).reshape(27 * channels, -1)  16.2 us
    all_to_all x1, starting transfers between devices, per_device(): lax.all_to_all(hidden, 'space', split_axis=0, concat_axis=1, tiled=True)  10.7 us
    unnamed x35, other arithmetic  7.14 us
    dot_general x1, matrix products, contract_last(): lax.dot_general(left_side, right_side, (((1,), (1,)), ((), ())), preferre...  7.13 us
  transfers between devices with their start and end apart: 5, of which 4 were waited for; matrix products, arithmetic and copies ran while one was open for 33% of the time, Pallas kernels for 0%

commit v1 on v0

--- a/solution.py
+++ b/solution.py
@@ -6,6 +6,12 @@
 C3 = 512
 WID = 128
 leak_slope = 0.3
+
+
+def add_all(array, mesh_axis):
+    pieces = lax.all_gather(array, mesh_axis, axis=0, tiled=False)
+    acc = pieces.sum(axis=0)
+    return acc
 
 
 def from_behind(block, axis, distance):
@@ -121,7 +127,7 @@
     cot_flat = gathered.reshape(C3, out_cells)
     weight_grad = contract_last(hidden_taps, cot_flat)
     tap_terms = jnp.dot(w_rows, cot_flat, preferred_element_type=jnp.float32)
-    grad_second = lax.psum(weight_grad, "dp").reshape(3, 3, 3, own_channels, C3)
+    grad_second = add_all(weight_grad, "dp").reshape(3, 3, 3, own_channels, C3)
 
     def spread(field):
         return jnp.stack(all_taps(field, row_len), 0).reshape(27 * own_channels, -1)

time: 219 us -> 190 us (0.87)
  waiting for transfers between devices: 82.9 us -> 34.5 us
  blocking collectives: 0 us -> 15.3 us
  local copies, waits for them, and re-layouts: 70.2 us -> 73.8 us
    psum x1 -> x0, waiting for transfers between devices: 42.7 us -> none  [per_device(): grad_second = lax.psum(weight_grad, 'dp').reshape(3, 3, 3, own_channels, C3)]
    all_gather x0 -> x1, blocking collectives: none -> 15.3 us  [add_all(): pieces = lax.all_gather(array, mesh_axis, axis=0, tiled=False)]
    all_to_all x1, waiting for transfers between devices: 2.99 us -> 0.01 us  [per_device(): lax.all_to_all(back_terms, 'space', split_axis=1, concat_axis=0, tiled=True)]
    another operation x11, local copies, waits for them, and re-layouts: 1.12 us -> 3.62 us  [plane_taps(): rows_out.append(jnp.stack(cols_out, -2))]
    ppermute x1, waiting for transfers between devices: 16.5 us -> 14.3 us  [from_behind(): return lax.ppermute(block, axis, route)]
    unnamed x29 -> x28, local copies, waits for them, and re-layouts: 34.1 us -> 32.5 us
  transfers between devices with their start and end apart: 5 -> 4, of which waited for: 4 -> 2; matrix products, arithmetic and copies ran while one was open for 33% -> 38% of each run, Pallas kernels for 0% -> 0%
where the time goes in v1:
time: 190 us; the launch traced here: 188 us
  local copies, waits for them, and re-layouts  73.8 us (39%)
  waiting for transfers between devices  34.5 us (18%)
  starting transfers between devices  18.8 us (10%)
  matrix products  17.2 us (9%)
  blocking collectives  15.3 us (8%)
  between operations  14.9 us (8%)
  other arithmetic  13.6 us (7%)
    unnamed x28, local copies, waits for them, and re-layouts  32.5 us
    all_to_all x1, waiting for transfers between devices, per_device(): lax.all_to_all(hidden, 'space', split_axis=0, concat_axis=1, tiled=True)  20.2 us
    reshape x1, local copies, waits for them, and re-layouts, per_device(): stacked = jnp.stack(collected, 0).reshape(27 * channels, -1)  16.2 us
    all_gather x1, blocking collectives, add_all(): pieces = lax.all_gather(array, mesh_axis, axis=0, tiled=False)  15.3 us
    ppermute x1, waiting for transfers between devices, from_behind(): return lax.ppermute(block, axis, route)  14.3 us
    all_to_all x1, starting transfers between devices, per_device(): lax.all_to_all(hidden, 'space', split_axis=0, concat_axis=1, tiled=True)  10 us
    unnamed x35, other arithmetic  7.03 us
    another operation x1, local copies, waits for them, and re-layouts, per_device(): stacked = jnp.stack(collected, 0).reshape(27 * channels, -1)  6.8 us
  transfers between devices with their start and end apart: 4, of which 2 were waited for; matrix products, arithmetic and copies ran while one was open for 38% of the time, Pallas kernels for 0%

profile of v1, /device:TPU:8, one launch (start us, length us, event | category | flops | bytes accessed | tf_op | source)
XLA Modules:
  0.0 188.1 jit_solution(14873679694465059724)
XLA Ops:
  7.2 2.9 %copy.103 = bf16[1,128,2,16,256]{4,1,3,2,0:T(8,128)(2,1)S(1)} copy(bf16[1,128,2,16,256]{4,3,2,1,0:T(8,128)(2,1)} %param.4) | data formatting | bytes 4194304 | tf_op args[0]
  10.1 1.1 slice_bitcast_fusion
  11.2 1.9 %collective-permute-start = (bf16[128,1,4,4,256]{4,0,3,2,1:T(8,128)(2,1)S(1)}, bf16[128,1,4,4,256]{4,0,3,2,1:T(8,128)(2,1)}, u32[]{:S(2)}, u32[]{:S(2)}) collective-permute-start(bf16[128,1,4,4,256]{4,0,3,2,1:T(8,128)(2,1)S(1)} %get-tuple-element.34), channel_id=1, source_target_pairs={{0,1},{1,2},{2,3},{3,4},{4,5},{5,6},{6,7},{7,8},{8,9},{9,10},{10,1... | collective-permute-start | bytes 3145736 | tf_op jit(solution)/shard_map/ppermute | solution.py:20
  14.7 1.4 slice_bitcast_fusion.58
  16.6 14.3 %collective-permute-done = bf16[128,1,4,4,256]{4,0,3,2,1:T(8,128)(2,1)} collective-permute-done((bf16[128,1,4,4,256]{4,0,3,2,1:T(8,128)(2,1)S(1)}, bf16[128,1,4,4,256]{4,0,3,2,1:T(8,128)(2,1)}, u32[]{:S(2)}, u32[]{:S(2)}) %collective-permute-start) | collective-permute-done | bytes 1048608 | tf_op jit(solution)/shard_map/ppermute | solution.py:20
  32.0 1.4 slice_bitcast_fusion.72
  35.3 6.8 %copy.104 = bf16[27,128,1,2,2,256]{5,4,3,1,0,2:T(2,128)(2,1)} copy(bf16[27,128,1,2,2,256]{5,1,4,3,2,0:T(8,128)(2,1)S(1)} %fusion.33) | data formatting | bytes 14155776 | tf_op jit(solution)/shard_map/stack | solution.py:116
  42.1 16.2 %reshape.233 = bf16[3456,1024]{1,0:T(8,128)(2,1)} reshape(bf16[27,128,1,2,2,256]{5,4,3,1,0,2:T(2,128)(2,1)} %copy.104) | data formatting | bytes 14155776 | tf_op jit(solution)/shard_map/reshape | solution.py:116
  58.3 6.2 %fusion.2 = (bf16[256,1024]{0,1:T(8,128)(2,1)S(1)}, f32[1024,256]{1,0:T(8,128)}) fusion(bf16[3456,1024]{1,0:T(8,128)(2,1)} %reshape.233, bf16[3456,256]{1,0:T(8,128)(2,1)S(1)} %bitcast.643), kind=kOutput, calls=%fused_computation.10 | convolution fusion | flops 1814036480 | bytes 10420224 | tf_op jit(solution)/shard_map/dot_general | solution.py:89
  64.4 1.1 copy.105
  65.5 10.0 %all-to-all-start = ((bf16[256,1,4,256]{3,2,1,0:T(4,128)(2,1)}), bf16[256,1,4,256]{3,2,1,0:T(4,128)(2,1)S(1)}, u32[]{:S(2)}, u32[]{:S(2)}) async-start(bf16[256,1,4,256]{3,2,1,0:T(4,128)(2,1)} %copy.105), calls=%async_computation | async-start | bytes 1048576 | tf_op jit(solution)/shard_map/all_to_all | solution.py:119
  75.6 1.6 copy.142
  77.3 20.2 %all-to-all-done = bf16[256,1,4,256]{3,2,1,0:T(4,128)(2,1)S(1)} async-done(((bf16[256,1,4,256]{3,2,1,0:T(4,128)(2,1)}), bf16[256,1,4,256]{3,2,1,0:T(4,128)(2,1)S(1)}, u32[]{:S(2)}, u32[]{:S(2)}) %all-to-all-start) | async-done | bytes 524320 | tf_op jit(solution)/shard_map/all_to_all | solution.py:119
  116.6 16.7 %copy.149 = bf16[64,8,32,256]{3,1,2,0:T(8,128)(2,1)} copy(bf16[64,8,32,256]{3,2,1,0:T(8,128)(2,1)} %bitcast.646) | data formatting | bytes 16777216
  133.3 4.7 %fusion.41 = f32[108,8192]{1,0:T(8,128)S(1)} fusion(bf16[108,512]{1,0:T(8,128)(2,1)S(1)} %reshape.238, bf16[512,8192]{1,0:T(8,128)(2,1)} %bitcast.644), kind=kOutput, calls=%fused_computation.302 | convolution fusion | flops 905969664 | bytes 12038144 | tf_op jit(solution)/shard_map/dot_general | solution.py:129
  141.9 1.1 copy.140
  143.0 6.8 %all-to-all-start.1 = ((bf16[4,64,4,256]{3,0,2,1:T(4,128)(2,1)}), bf16[4,64,4,256]{3,0,2,1:T(4,128)(2,1)S(1)}, u32[]{:S(2)}, u32[]{:S(2)}) async-start(bf16[4,64,4,256]{3,0,2,1:T(4,128)(2,1)} %bitcast.261), calls=%async_computation.1 | async-start | bytes 1048576 | tf_op jit(solution)/shard_map/all_to_all | solution.py:140
  150.4 1.8 copy.111
  152.4 1.2 copy.150
  153.6 6.3 %convolution_bitcast_fusion = f32[1,108,512]{2,1,0:T(8,128)S(1)} fusion(bf16[108,8192]{1,0:T(8,128)(2,1)S(1)} %bitcast.648, bf16[512,8192]{1,0:T(8,128)(2,1)} %bitcast.645), kind=kOutput, calls=%fused_computation | convolution fusion | flops 905969664 | bytes 10379264 | tf_op jit(solution)/shard_map/dot_general | solution.py:95
  160.0 15.3 %all-gather.2 = f32[4,108,512]{2,1,0:T(8,128)} all-gather(f32[1,108,512]{2,1,0:T(8,128)S(1)} %convolution_bitcast_fusion), channel_id=3, replica_groups=mesh['dp'=4,'space'=64] {'dp'}, dimensions={0}, use_global_device_ids=true | all-gather | bytes 1105920 | tf_op jit(solution)/shard_map/all_gather | solution.py:12
  175.3 2.0 %reduce_sum.9 = f32[108,512]{1,0:T(8,128)} reduce(f32[4,108,512]{2,1,0:T(8,128)} %all-gather.2, f32[]{:T(128)} %constant.147.clone.1), dimensions={0}, to_apply=%region_0.1 | reduce | flops 165888 | bytes 1105924 | tf_op jit(solution)/shard_map/reduce_sum | solution.py:13
  177.2 1.7 reshape.237
  179.5 1.8 fusion
  (144 shorter events, 28.9 us)
Async XLA Ops:
  7.2 51.1 %copy-start = (bf16[3,3,3,128,256]{4,3,2,1,0:T(8,128)(2,1)S(1)}, bf16[3,3,3,128,256]{4,3,2,1,0:T(8,128)(2,1)}, u32[]{:S(2)}) copy-start(bf16[3,3,3,128,256]{4,3,2,1,0:T(8,128)(2,1)} %param.5) | copy-start | bytes 5308420
  7.2 109.4 %all-gather.5.cloned.1.call-start = ((), (), s32[]{:S(2)}) async-start(), calls=%async_computation.2 | async-start | bytes 8519680 | tf_op jit(solution)/shard_map/all_gather | solution.py:126
  11.2 19.7 %collective-permute-start = (bf16[128,1,4,4,256]{4,0,3,2,1:T(8,128)(2,1)S(1)}, bf16[128,1,4,4,256]{4,0,3,2,1:T(8,128)(2,1)}, u32[]{:S(2)}, u32[]{:S(2)}) collective-permute-start(bf16[128,1,4,4,256]{4,0,3,2,1:T(8,128)(2,1)S(1)} %get-tuple-element.34), channel_id=1, source_target_pairs={{0,1},{1,2},{2,3},{3,4},{4,5},{5,6},{6,7},{7,8},{8,9},{9,10},{10,1... | collective-permute-start | bytes 3145736 | tf_op jit(solution)/shard_map/ppermute | solution.py:20
  58.3 17.3 %copy-start.2 = (bf16[3,3,3,4,512]{4,3,2,1,0:T(4,128)(2,1)S(1)}, bf16[3,3,3,4,512]{4,3,2,1,0:T(4,128)(2,1)}, u32[]{:S(2)}) copy-start(bf16[3,3,3,4,512]{4,3,2,1,0:T(4,128)(2,1)} %param.6) | copy-start | bytes 331780
  65.5 32.0 %all-to-all-start = ((bf16[256,1,4,256]{3,2,1,0:T(4,128)(2,1)}), bf16[256,1,4,256]{3,2,1,0:T(4,128)(2,1)S(1)}, u32[]{:S(2)}, u32[]{:S(2)}) async-start(bf16[256,1,4,256]{3,2,1,0:T(4,128)(2,1)} %copy.105), calls=%async_computation | async-start | bytes 1048576 | tf_op jit(solution)/shard_map/all_to_all | solution.py:119
  143.0 35.9 %all-to-all-start.1 = ((bf16[4,64,4,256]{3,0,2,1:T(4,128)(2,1)}), bf16[4,64,4,256]{3,0,2,1:T(4,128)(2,1)S(1)}, u32[]{:S(2)}, u32[]{:S(2)}) async-start(bf16[4,64,4,256]{3,0,2,1:T(4,128)(2,1)} %bitcast.261), calls=%async_computation.1 | async-start | bytes 1048576 | tf_op jit(solution)/shard_map/all_to_all | solution.py:140
  160.0 21.3 %copy-start.1 = (bf16[3,3,3,128,256]{4,3,2,1,0:T(8,128)(2,1)S(1)}, bf16[3,3,3,128,256]{4,3,2,1,0:T(8,128)(2,1)}, u32[]{:S(2)}) copy-start(bf16[3,3,3,128,256]{4,3,2,1,0:T(8,128)(2,1)} %param.5) | copy-start | bytes 5308420
Sparse Core Ops, SparseCore 0:
  13.3 95.7 all-gather.4
